TPU v7x, 32 devices: a whole 2x2x4 slice. The times are simulated.
32 devices in a mesh: grp: 4 (over y, x), side: 2 (over core), seq: 4 (over z).
Axes of the slice: x: 2, y: 2, z: 4, core: 2. Of those that a mesh axis runs over, the one named last changes fastest.
Arguments:
- queries: bfloat16 [2, 4, 256, 64, 576], P('side', 'grp', 'seq'), may hold values from -48 to 48
- stream_rows: bfloat16 [2, 4, 256, 576], P('side', 'grp', 'seq'), may hold values from -6 to 6
- span_latents: bfloat16 [4, 256, 576], P('grp', 'seq'), may hold values from -6 to 6
- decode_cache: bfloat16 [65536, 576], P(('grp', 'seq')), may hold values from -6 to 6
- cache_lengths: int32 [16, 64], P(('grp', 'seq')), may hold values from 1 to 256, 4096 in all within a row
- block_owner: int32 [32, 1], replicated, may hold values from 0 to 15; in each aligned block of 32 rows (0 to 31, 32 to 63, ...) at most 4 rows name the same one
- block_request: int32 [32], replicated, may hold values from 0 to 63
Outputs:
- attended: bfloat16 [2, 4, 256, 64, 512], P('side', 'grp', 'seq')
Inputs may be any that keep to these rules, and one draw needn't show every extreme that they name: Each row of cache_lengths sums to 4096; a device's requests take consecutive rows of its 4096 resident rows in order. `block_owner`: decode devices are numbered grp index * 4 + seq index; no device receives more than 4 blocks.
All inputs are finite; a program needn't handle non-finite values.
Results may differ from a plain program's by a relative error of at most 0.0048.
Values may be sent and summed in bfloat16 or wider, within the bound.
No kernel may reach another device: no remote copies, remote signals or barrier semaphores. Data moves between devices by JAX's collectives and lax.ppermute only.
A program may use at most 128 MiB of HBM per device.

v0:
```python
import math
import jax
import jax.numpy as jnp
from jax import lax
from jax.sharding import PartitionSpec as P

LAT = 512
ROPE = 64
NOPE = 128
BLOCK = 32
MOSTLEN = 256


def shifted(block, axis, distance):
    devices = range(lax.axis_size(axis))
    route = [(i - distance, i) for i in devices if i - distance in devices]
    return lax.ppermute(block, axis, route)


def masked_weights(score_rows, allowed):
    masked = jnp.where(allowed, score_rows, -jnp.inf)
    largest = jnp.max(masked, axis=-1, keepdims=True)
    lifted = jnp.exp(masked - largest)
    return (lifted / jnp.sum(lifted, axis=-1, keepdims=True)).astype(jnp.bfloat16)


def prefill_side(own_query, key_rows, first_row):
    row_count, head_count, row_width = own_query.shape
    span_rows = key_rows.shape[0] // 2
    factor = 1.0 / math.sqrt(NOPE + ROPE)
    head_group = min(head_count, max(1, 512 // row_count))
    allowed = (jnp.arange(2 * span_rows) - span_rows)[None, None, :] <= (
        first_row + jnp.arange(row_count)
    )[:, None, None]
    grouped = jnp.transpose(
        own_query.reshape(row_count, head_count // head_group, head_group, row_width), (1, 0, 2, 3)
    )
    value_rows = key_rows[:, :LAT]

    def one_group(group_query):
        scored = (
            jnp.einsum("rhw,kw->rhk", group_query, key_rows, preferred_element_type=jnp.float32)
            * factor
        )
        weights = masked_weights(scored, allowed)
        return jnp.einsum(
            "rhk,kl->rhl", weights, value_rows, preferred_element_type=jnp.float32
        ).astype(jnp.bfloat16)

    results = lax.map(one_group, grouped)
    return jnp.transpose(results, (1, 0, 2, 3)).reshape(row_count, head_count, LAT)


def decode_side(own_query, own_latent, pool_rows, lengths, arrived, arrived_allowed):
    row_count = own_query.shape[0]
    factor = 1.0 / math.sqrt(NOPE + ROPE)
    offsets = jnp.cumsum(lengths) - lengths
    padded = jnp.concatenate(
        [pool_rows, jnp.zeros((MOSTLEN, pool_rows.shape[1]), pool_rows.dtype)], 0
    )
    row_index = offsets[:, None] + jnp.arange(MOSTLEN, dtype=jnp.int32)[None, :]
    windows = jnp.take(padded, row_index, axis=0)
    resident = (
        jnp.einsum("rhw,rtw->rht", own_query, windows, preferred_element_type=jnp.float32) * factor
    )
    incoming = (
        jnp.einsum("rhw,kw->rhk", own_query, arrived, preferred_element_type=jnp.float32) * factor
    )
    itself = (
        jnp.einsum("rhw,rw->rh", own_query, own_latent, preferred_element_type=jnp.float32)[
            :, :, None
        ]
        * factor
    )
    scored = jnp.concatenate([resident, incoming, itself], -1)
    resident_allowed = jnp.arange(MOSTLEN)[None, :] < lengths[:, None]
    allowed = jnp.concatenate(
        [resident_allowed, arrived_allowed, jnp.ones((row_count, 1), jnp.bool_)], -1
    )[:, None, :]
    weights = masked_weights(scored, allowed)
    split_point = MOSTLEN + arrived.shape[0]
    context = jnp.einsum(
        "rht,rtl->rhl",
        weights[:, :, :MOSTLEN],
        windows[:, :, :LAT],
        preferred_element_type=jnp.float32,
    )
    context = context + jnp.einsum(
        "rhk,kl->rhl",
        weights[:, :, MOSTLEN:split_point],
        arrived[:, :LAT],
        preferred_element_type=jnp.float32,
    )
    context = context + weights[:, :, split_point:].astype(jnp.float32) * own_latent[
        :, None, :LAT
    ].astype(jnp.float32)
    return context.astype(jnp.bfloat16)


def local(
    queries, stream_rows, span_latents, decode_cache, cache_lengths, block_owner, block_request
):
    own_query = queries[0, 0]
    own_stream = stream_rows[0, 0]
    own_span = span_latents[0]
    row_count = own_query.shape[0]
    row_width = own_stream.shape[1]
    seq_index = lax.axis_index("seq")
    grp_index = lax.axis_index("grp")
    side_index = lax.axis_index("side")
    seq_count = lax.axis_size("seq")
    per_device = row_count // BLOCK
    capacity = 2 * per_device
    owners = block_owner[:, 0]
    total_blocks = owners.shape[0]
    my_owner = grp_index * seq_count + seq_index
    earlier, current = (
        lax.all_gather(own_stream, "seq", axis=0, tiled=True),
        lax.all_gather(own_span, "seq", axis=0, tiled=True),
    )
    handed = shifted(own_stream, "side", 1)
    landed = lax.all_gather(handed, ("grp", "seq"), axis=0, tiled=True)
    landed = landed.reshape(total_blocks, BLOCK, row_width)
    block_ids = jnp.arange(total_blocks, dtype=jnp.int32)
    order_key = jnp.where(owners == my_owner, block_ids, total_blocks + block_ids)
    picked = jnp.argsort(order_key)[:capacity]
    present = owners[picked] == my_owner
    requests = block_request[picked]
    arrived = landed[picked].reshape(capacity * BLOCK, row_width)
    arrived_allowed = jnp.repeat(
        present[None, :] & (requests[None, :] == jnp.arange(row_count)[:, None]), BLOCK, axis=1
    )
    first_row = seq_index * row_count
    key_rows = jnp.concatenate([earlier, current], 0)
    context = lax.cond(
        side_index == 0,
        lambda: prefill_side(own_query, key_rows, first_row),
        lambda: decode_side(
            own_query, own_stream, decode_cache, cache_lengths[0], arrived, arrived_allowed
        ),
    )
    return context[None, None]


def solution(mesh):
    return jax.shard_map(
        local,
        mesh=mesh,
        in_specs=(
            P("side", "grp", "seq", None, None),
            P("side", "grp", "seq", None),
            P("grp", "seq", None),
            P(("grp", "seq"), None),
            P(("grp", "seq"), None),
            P(),
            P(),
        ),
        out_specs=P("side", "grp", "seq", None, None),
        check_vma=False,
    )
```

profile of v0, /device:TPU:1, one launch (start us, length us, event | category | flops | bytes accessed | tf_op | source)
XLA Modules:
  0.0 228.1 jit_solution(6818129309431499111)
XLA Ops:
  6.5 0.0 all-gather.4.cloned.1.call-start
  6.5 1.3 collective-permute-start
  7.8 2.1 collective-permute-done
  9.9 0.0 copy-start.4
  9.9 0.6 copy-done.4
  10.5 0.0 all-gather.4.cloned.1.call-update
  10.6 0.7 compare_select_fusion.3
  11.2 1.7 sort.17
  12.9 14.4 %all-gather = bf16[1,1,256,576]{3,2,1,0:T(8,128)(2,1)S(1)} all-gather(bf16[1,1,64,576]{3,2,1,0:T(8,128)(2,1)} %param.12), channel_id=2, replica_groups=mesh['grp'=4,'side'=2,'seq'=4] {'seq'}, dimensions={2}, use_global_device_ids=true | all-gather | bytes 368640 | tf_op jit(solution)/shard_map/all_gather | solution.py:118
  27.3 11.7 %all-gather.1 = bf16[1,256,576]{2,1,0:T(8,128)(2,1)S(1)} all-gather(bf16[1,64,576]{2,1,0:T(8,128)(2,1)} %param.13), channel_id=3, replica_groups=mesh['grp'=4,'side'=2,'seq'=4] {'seq'}, dimensions={1}, use_global_device_ids=true | all-gather | bytes 368640 | tf_op jit(solution)/shard_map/all_gather | solution.py:119
  38.9 0.1 pad_maximum_fusion
  39.0 28.3 %all-gather.4.cloned.1.call-done = bf16[1024,576]{1,0:T(8,128)(2,1)} async-done(((bf16[64,576]{1,0:T(8,128)(2,1)}), bf16[1024,576]{1,0:T(8,128)(2,1)}) %all-gather.4.cloned.1.call-update) | async-done | bytes 1179664 | tf_op jit(solution)/shard_map/all_gather | solution.py:122
  67.4 151.9 %conditional.1 = (bf16[1,1,64,64,512]{4,3,2,1,0:T(8,128)(2,1)S(1)}) conditional(s32[]{:T(128)} %convert_element_type.20, (s32[1,64]{1,0:T(1,128)}, s32[32]{0:T(128)}, bf16[4096,576]{0,1:T(8,128)(2,1)}, bf16[1,1,64,64,576]{4,3,2,1,0:T(8,128)(2,1)}, bf16[1024,576]{1,0:T(8,128)(2,1)}, /*index=5*/bf16[64,576]{1,0:T(8,128)(2,1)}, ...), branch_computations={%region_1.5_spmd.clone, %region_5.10_spmd} | conditional | flops 3458017280 | bytes 214683328 | solution.py:135
  67.4 0.7 copy.48
  68.1 0.1 reduce-window.8
  68.2 0.1 reduce
  68.3 0.7 bitcast_subtract_fusion
  69.0 0.1 fusion.47
  69.1 7.7 %copy.55 = bf16[4096,576]{1,0:T(8,128)(2,1)} copy(bf16[4096,576]{0,1:T(8,128)(2,1)} %get-tuple-element.198) | data formatting | bytes 9437184 | tf_op jit(solution)/shard_map
  76.8 5.4 %concatenate.14 = bf16[4352,576]{1,0:T(8,128)(2,1)} pad(bf16[4096,576]{1,0:T(8,128)(2,1)} %copy.55, bf16[]{:T(256)} %constant.39.clone.1), padding=0_256x0_0 | pad | bytes 9732098 | tf_op jit(solution)/shard_map/cond/branch_0_fun/concatenate | solution.py:58
  82.1 72.1 %gather_fusion = bf16[16384,576]{1,0:T(8,128)(2,1)} fusion(bf16[4352,576]{1,0:T(8,128)(2,1)} %concatenate.14, s32[16384]{0:T(1024)S(1)} %broadcast_clamp_fusion), kind=kCustom, calls=%fused_computation | custom fusion | bytes 37814272 | tf_op jit(solution)/shard_map/cond/branch_0_fun/jit(_take)/gather | solution.py:62
  154.2 0.1 fusion.50
  154.3 18.1 %broadcast_select_fusion = bf16[64,256,576]{2,1,0:T(8,128)(2,1)} fusion(bf16[64,256,576]{2,1,0:T(8,128)(2,1)} %bitcast.97, pred[64,256]{1,0:T(8,128)(4,1)S(1)} %fusion.50), kind=kLoop, calls=%fused_computation.29 | loop fusion | flops 9437184 | bytes 37765120 | tf_op jit(solution)/shard_map/cond/branch_0_fun/jit(_take)/select_n | solution.py:62
  172.4 0.0 copy-start
  172.4 13.1 %multiply_bitcast_fusion = f32[64,64,256]{2,1,0:T(8,128)} fusion(bf16[64,256,576]{2,1,0:T(8,128)(2,1)} %broadcast_select_fusion, bf16[1,1,64,64,576]{4,3,2,1,0:T(8,128)(2,1)} %get-tuple-element.106), kind=kOutput, calls=%fused_computation.45 | convolution fusion | flops 1209008128 | bytes 27787264 | tf_op jit(solution)/shard_map/cond/branch_0_fun/rhw,rtw->rht/dot_general | solution.py:64
  185.6 0.0 copy-done
  185.6 0.6 gather_fusion.2
  186.2 0.0 copy-done.1
  186.2 0.6 gather_fusion.3
  186.9 0.1 compare_and_fusion
  187.0 0.1 copy.47
  187.1 0.0 copy-done.5
  187.1 0.1 iota_compare_fusion
  187.2 2.0 gather_fusion.1
  189.2 0.0 slice-start.1
  189.2 4.2 %multiply_bitcast_fusion.1 = f32[64,64,128]{2,1,0:T(8,128)S(1)} fusion(bf16[128,576,1]{1,0,2:T(8,128)(2,1)S(1)} %bitcast.103, bf16[1,1,64,64,576]{4,3,2,1,0:T(8,128)(2,1)} %get-tuple-element.106), kind=kOutput, calls=%fused_computation.49 | convolution fusion | flops 604504064 | bytes 6963200 | tf_op jit(solution)/shard_map/cond/branch_0_fun/rhw,kw->rhk/dot_general | solution.py:67
  193.4 0.0 slice-done
  193.4 0.0 copy-done.3
  193.4 0.0 slice-done.1
  193.4 1.7 fusion.30
  195.1 2.0 copy.51
  197.2 4.3 %fusion.58 = (f32[64,64]{1,0:T(8,128)S(1)}, f32[64,64,385]{2,1,0:T(8,128)S(1)}) fusion(f32[64,64,1]{2,1,0:T(8,128)} %copy.51, f32[64,64,128]{2,1,0:T(8,128)S(1)} %multiply_bitcast_fusion.1, f32[64,64,256]{2,1,0:T(8,128)} %multiply_bitcast_fusion, pred[64,385]{1,0:T(8,128)(4,1)S(1)} %add_add_fusion), kind=kOutput, calls=%fused_computation.74 | output fusion | flops 7885184 | bytes 12656704 | tf_op jit(solution)/shard_map/cond/branch_0_fun/sub | solution.py:23
  201.5 0.8 divide_convert_fusion.2
  202.3 12.1 %fusion.28 = f32[64,64,512]{2,1,0:T(8,128)} fusion(bf16[64,256,576]{2,1,0:T(8,128)(2,1)} %broadcast_select_fusion, bf16[64,64,385]{2,1,0:T(8,128)(2,1)S(1)} %divide_convert_fusion.2), kind=kOutput, calls=%fused_computation.30 | convolution fusion | flops 1073741824 | bytes 27262976 | tf_op jit(solution)/shard_map/cond/branch_0_fun/rht,rtl->rhl/dot_general | solution.py:82
  214.4 0.6 convert_reduce_fusion
  215.1 4.2 %fusion.37 = bf16[1,1,64,64,512]{4,3,2,1,0:T(8,128)(2,1)S(1)} fusion(f32[64,64,512]{2,1,0:T(8,128)} %fusion.28, f32[64,512]{1,0:T(8,128)S(1)} %slice_convert_fusion, f32[64,64]{1,0:T(8,128)S(1)} %convert_reduce_fusion, bf16[64,64,385]{2,1,0:T(8,128)(2,1)S(1)} %divide_convert_fusion.2, bf16[128,576]{1,0:T(8,128)(2,1)S(1)} %bitcast.104), kind=kOutput, calls=%fused_computation.43 | convolution fusion | flops 545259520 | bytes 13926400 | tf_op jit(solution)/shard_map/cond/branch_0_fun/rhk,kl->rhl/dot_general | solution.py:88
  219.3 0.0 copy-start.2
  219.3 2.0 copy-done.2
  (17 shorter events, 0.1 us)
Async XLA Ops:
  6.5 60.8 %all-gather.4.cloned.1.call-start = ((), (), s32[]{:S(2)}) async-start(), calls=%async_computation | async-start | bytes 1392640 | tf_op jit(solution)/shard_map/all_gather | solution.py:122
  6.5 3.4 %collective-permute-start = (bf16[64,576]{1,0:T(8,128)(2,1)}, bf16[64,576]{1,0:T(8,128)(2,1)S(1)}, u32[]{:S(2)}, u32[]{:S(2)}) collective-permute-start(bf16[64,576]{1,0:T(8,128)(2,1)} %bitcast.105), channel_id=1, source_target_pairs={{0,4},{1,5},{2,6},{3,7},{8,12},{9,13},{10,14},{11,15},{16,20},{17,... | collective-permute-start | bytes 221192 | tf_op jit(solution)/shard_map/ppermute | solution.py:17
  9.9 0.6 copy-start.4
  172.4 13.1 %copy-start = (s32[32]{0:T(128)S(1)}, s32[32]{0:T(128)}, u32[]{:S(2)}) copy-start(s32[32]{0:T(128)} %get-tuple-element.112) | copy-start | bytes 388 | tf_op jit(solution)/shard_map/cond
  172.4 13.8 %copy-start.1 = (s32[32]{0:T(128)S(1)}, s32[32]{0:T(128)}, u32[]{:S(2)}) copy-start(s32[32]{0:T(128)} %get-tuple-element.116) | copy-start | bytes 388 | tf_op jit(solution)/shard_map/cond
  172.4 14.6 %copy-start.5 = (s32[1,64]{1,0:T(1,128)S(1)}, s32[1,64]{1,0:T(1,128)}, u32[]{:S(2)}) copy-start(s32[1,64]{1,0:T(1,128)} %get-tuple-element.107) | copy-start | bytes 772 | tf_op jit(solution)/shard_map/cond
  186.9 6.4 %slice-start = ((s8[5242880]{0:T(1024)(128)(4,1)}), s8[1048576]{0:T(1024)(128)(4,1)S(1)}, s32[]{:S(2)}) async-start(s8[5242880]{0:T(1024)(128)(4,1)} %bitcast.98), calls=%async_computation.1 | async-start | bytes 2097152 | tf_op jit(solution)/shard_map/cond
  186.9 6.4 %copy-start.3 = (bf16[64,576]{1,0:T(8,128)(2,1)S(1)}, bf16[64,576]{1,0:T(8,128)(2,1)}, u32[]{:S(2)}) copy-start(bf16[64,576]{1,0:T(8,128)(2,1)} %get-tuple-element.105) | copy-start | bytes 221188 | tf_op jit(solution)/shard_map/cond
  189.2 4.2 %slice-start.1 = ((s8[5242880]{0:T(1024)(128)(4,1)}), s8[4194304]{0:T(1024)(128)(4,1)S(1)}, s32[]{:S(2)}) async-start(s8[5242880]{0:T(1024)(128)(4,1)} %bitcast.98), calls=%async_computation.2 | async-start | bytes 8388608 | tf_op jit(solution)/shard_map/cond
  219.3 2.0 copy-start.2
Sparse Core Ops, SparseCore 0:
  10.7 56.6 all-gather.3
where the time goes:
time: 229 us; the launch traced here: 228 us
  local copies, waits for them, and re-layouts  94 us (41%)
  matrix products  35.3 us (15%)
  waiting for transfers between devices  30.4 us (13%)
  other arithmetic  27.5 us (12%)
  blocking collectives  26 us (11%)
  between operations  13.4 us (6%)
    gather x1, local copies, waits for them, and re-layouts, decode_side(): windows = jnp.take(padded, row_index, axis=0)  72.1 us
    all_gather x1, waiting for transfers between devices, local(): landed = lax.all_gather(handed, ('grp', 'seq'), axis=0, tiled=True)  28.3 us
    select_n x1, other arithmetic, decode_side(): windows = jnp.take(padded, row_index, axis=0)  18.1 us
    all_gather x1, blocking collectives, local(): lax.all_gather(own_stream, 'seq', axis=0, tiled=True)  14.4 us
    dot_general x1, matrix products, decode_side(): jnp.einsum('rhw,rtw->rht', own_query, windows, preferred_element_type=jnp...  13.1 us
    dot_general x1, matrix products, decode_side(): jnp.einsum('rht,rtl->rhl', weights[:, :, :MOSTLEN], windows[:, :, :LAT],...  12.1 us
    all_gather x1, blocking collectives, local(): lax.all_gather(own_span, 'seq', axis=0, tiled=True)  11.7 us
    another operation x2, local copies, waits for them, and re-layouts  8.39 us
  transfers between devices with their start and end apart: 2, of which 2 were waited for; matrix products, arithmetic and copies ran while one was open for 1% of the time, Pallas kernels for 0%

commit v1 on v0

--- a/solution.py
+++ b/solution.py
@@ -119,7 +119,29 @@
         lax.all_gather(own_span, "seq", axis=0, tiled=True),
     )
     handed = shifted(own_stream, "side", 1)
-    landed = lax.all_gather(handed, ("grp", "seq"), axis=0, tiled=True)
+    ways, here, lap = (
+        lax.axis_size(("grp", "seq")),
+        lax.axis_index(("grp", "seq")),
+        handed.shape[0],
+    )
+    shape = [n * ways if d == 0 else n for d, n in enumerate(handed.shape)]
+    full = lax.dynamic_update_slice_in_dim(
+        jnp.zeros(shape, handed.dtype), handed, here * lap, axis=0
+    )
+    going_up = going_down = handed
+    for far in range(1, ways // 2 + 1):
+        going_up = lax.ppermute(
+            going_up, ("grp", "seq"), [(d, (d + 1) % ways) for d in range(ways)]
+        )
+        full = lax.dynamic_update_slice_in_dim(full, going_up, (here - far) % ways * lap, axis=0)
+        if 2 * far < ways:
+            going_down = lax.ppermute(
+                going_down, ("grp", "seq"), [(d, (d - 1) % ways) for d in range(ways)]
+            )
+            full = lax.dynamic_update_slice_in_dim(
+                full, going_down, (here + far) % ways * lap, axis=0
+            )
+    landed = full
     landed = landed.reshape(total_blocks, BLOCK, row_width)
     block_ids = jnp.arange(total_blocks, dtype=jnp.int32)
     order_key = jnp.where(owners == my_owner, block_ids, total_blocks + block_ids)

time: 229 us -> 249 us (1.087)
  starting transfers between devices: 1.28 us -> 37.6 us
  waiting for transfers between devices: 30.4 us -> 17.2 us
  between operations: 13.4 us -> 0.3 us
  local copies, waits for them, and re-layouts: 94 us -> 103 us
    ppermute x0 -> x15, starting transfers between devices: none -> 36.3 us  [the longest x7 34.2 us: local(): lax.ppermute(going_down, ('grp', 'seq'), [(d, (d - 1) % ways) for d in ra...]
    all_gather x1 -> x0, waiting for transfers between devices: 28.3 us -> none  [local(): landed = lax.all_gather(handed, ('grp', 'seq'), axis=0, tiled=True)]
    ppermute x0 -> x15, waiting for transfers between devices: none -> 15.1 us  [the longest x8 12.4 us: local(): lax.ppermute(going_up, ('grp', 'seq'), [(d, (d + 1) % ways) for d in rang...]
    dynamic_update_slice x0 -> x16, local copies, waits for them, and re-layouts: none -> 11.7 us  [the longest x8 5.71 us: local(): lax.dynamic_update_slice_in_dim(full, going_up, (here - far) % ways * lap...]
  transfers between devices with their start and end apart: 2 -> 16, of which waited for: 2 -> 7; matrix products, arithmetic and copies ran while one was open for 1% -> 1% of each run, Pallas kernels for 0% -> 0%
where the time goes in v1:
time: 249 us; the launch traced here: 248 us
  local copies, waits for them, and re-layouts  103 us (41%)
  matrix products  37.7 us (15%)
  starting transfers between devices  37.6 us (15%)
  other arithmetic  27.1 us (11%)
  blocking collectives  24.7 us (10%)
  waiting for transfers between devices  17.2 us (7%)
    gather x1, local copies, waits for them, and re-layouts, decode_side(): windows = jnp.take(padded, row_index, axis=0)  72.1 us
    ppermute x7, starting transfers between devices, local(): lax.ppermute(going_down, ('grp', 'seq'), [(d, (d - 1) % ways) for d in ra...  34.2 us
    select_n x1, other arithmetic, decode_side(): windows = jnp.take(padded, row_index, axis=0)  18.1 us
    dot_general x1, matrix products, decode_side(): jnp.einsum('rhw,rtw->rht', own_query, windows, preferred_element_type=jnp...  13.1 us
    all_gather x1, blocking collectives, local(): lax.all_gather(own_stream, 'seq', axis=0, tiled=True)  12.7 us
    ppermute x8, waiting for transfers between devices, local(): lax.ppermute(going_up, ('grp', 'seq'), [(d, (d + 1) % ways) for d in rang...  12.4 us
    dot_general x1, matrix products, decode_side(): jnp.einsum('rht,rtl->rhl', weights[:, :, :MOSTLEN], windows[:, :, :LAT],...  12.1 us
    all_gather x1, blocking collectives, local(): lax.all_gather(own_span, 'seq', axis=0, tiled=True)  12.1 us
  transfers between devices with their start and end apart: 16, of which 7 were waited for; matrix products, arithmetic and copies ran while one was open for 1% of the time, Pallas kernels for 0%

profile of v1, /device:TPU:1, one launch (start us, length us, event | category | flops | bytes accessed | tf_op | source)
XLA Modules:
  0.0 248.2 jit_solution(9310816566426398019)
XLA Ops:
  0.0 1.3 collective-permute-start
  1.3 2.1 collective-permute-done
  3.4 2.1 collective-permute-start.1
  5.5 3.9 %collective-permute-start.2 = (bf16[64,576]{1,0:T(8,128)(2,1)S(1)}, bf16[64,576]{1,0:T(8,128)(2,1)S(1)}, u32[]{:S(2)}, u32[]{:S(2)}) collective-permute-start(bf16[64,576]{1,0:T(8,128)(2,1)S(1)} %collective-permute-done), channel_id=1, source_target_pairs={{0,27},{1,0},{2,1},{3,2},{8,3},{9,8},{10,9},{11,10},{16,11},{17,16... | collective-permute-start | bytes 221192 | tf_op jit(solution)/shard_map/ppermute | solution.py:138
  9.4 2.7 %collective-permute-done.1 = bf16[64,576]{1,0:T(8,128)(2,1)S(1)} collective-permute-done((bf16[64,576]{1,0:T(8,128)(2,1)S(1)}, bf16[64,576]{1,0:T(8,128)(2,1)S(1)}, u32[]{:S(2)}, u32[]{:S(2)}) %collective-permute-start.1) | collective-permute-done | bytes 73760 | tf_op jit(solution)/shard_map/ppermute | solution.py:133
  12.1 5.1 %collective-permute-start.4 = (bf16[64,576]{1,0:T(8,128)(2,1)S(1)}, bf16[64,576]{1,0:T(8,128)(2,1)S(1)}, u32[]{:S(2)}, u32[]{:S(2)}) collective-permute-start(bf16[64,576]{1,0:T(8,128)(2,1)S(1)} %collective-permute-done.2), channel_id=1, source_target_pairs={{0,27},{1,0},{2,1},{3,2},{8,3},{9,8},{10,9},{11,10},{16,11},{17,16... | collective-permute-start | bytes 221192 | tf_op jit(solution)/shard_map/ppermute | solution.py:138
  17.1 1.9 collective-permute-done.3
  19.1 5.1 %collective-permute-start.6 = (bf16[64,576]{1,0:T(8,128)(2,1)S(1)}, bf16[64,576]{1,0:T(8,128)(2,1)S(1)}, u32[]{:S(2)}, u32[]{:S(2)}) collective-permute-start(bf16[64,576]{1,0:T(8,128)(2,1)S(1)} %collective-permute-done.4), channel_id=1, source_target_pairs={{0,27},{1,0},{2,1},{3,2},{8,3},{9,8},{10,9},{11,10},{16,11},{17,16... | collective-permute-start | bytes 221192 | tf_op jit(solution)/shard_map/ppermute | solution.py:138
  24.2 1.9 collective-permute-done.5
  26.7 1.6 sort.17
  28.3 5.1 %collective-permute-start.8 = (bf16[64,576]{1,0:T(8,128)(2,1)S(1)}, bf16[64,576]{1,0:T(8,128)(2,1)S(1)}, u32[]{:S(2)}, u32[]{:S(2)}) collective-permute-start(bf16[64,576]{1,0:T(8,128)(2,1)S(1)} %collective-permute-done.6), channel_id=1, source_target_pairs={{0,27},{1,0},{2,1},{3,2},{8,3},{9,8},{10,9},{11,10},{16,11},{17,16... | collective-permute-start | bytes 221192 | tf_op jit(solution)/shard_map/ppermute | solution.py:138
  33.6 1.2 collective-permute-done.8
  34.9 5.5 %collective-permute-start.10 = (bf16[64,576]{1,0:T(8,128)(2,1)S(1)}, bf16[64,576]{1,0:T(8,128)(2,1)S(1)}, u32[]{:S(2)}, u32[]{:S(2)}) collective-permute-start(bf16[64,576]{1,0:T(8,128)(2,1)S(1)} %collective-permute-done.8), channel_id=1, source_target_pairs={{0,27},{1,0},{2,1},{3,2},{8,3},{9,8},{10,9},{11,10},{16,11},{17,16... | collective-permute-start | bytes 221192 | tf_op jit(solution)/shard_map/ppermute | solution.py:138
  40.4 12.7 %all-gather = bf16[1,1,256,576]{3,2,1,0:T(8,128)(2,1)S(1)} all-gather(bf16[1,1,64,576]{3,2,1,0:T(8,128)(2,1)} %param.12), channel_id=2, replica_groups=mesh['grp'=4,'side'=2,'seq'=4] {'seq'}, dimensions={2}, use_global_device_ids=true | all-gather | bytes 368640 | tf_op jit(solution)/shard_map/all_gather | solution.py:118
  53.1 4.9 %collective-permute-start.12 = (bf16[64,576]{1,0:T(8,128)(2,1)S(1)}, bf16[64,576]{1,0:T(8,128)(2,1)S(1)}, u32[]{:S(2)}, u32[]{:S(2)}) collective-permute-start(bf16[64,576]{1,0:T(8,128)(2,1)S(1)} %collective-permute-done.10), channel_id=1, source_target_pairs={{0,27},{1,0},{2,1},{3,2},{8,3},{9,8},{10,9},{11,10},{16,11},{17,16... | collective-permute-start | bytes 221192 | tf_op jit(solution)/shard_map/ppermute | solution.py:138
  57.9 12.1 %all-gather.1 = bf16[1,256,576]{2,1,0:T(8,128)(2,1)S(1)} all-gather(bf16[1,64,576]{2,1,0:T(8,128)(2,1)} %param.13), channel_id=3, replica_groups=mesh['grp'=4,'side'=2,'seq'=4] {'seq'}, dimensions={1}, use_global_device_ids=true | all-gather | bytes 368640 | tf_op jit(solution)/shard_map/all_gather | solution.py:119
  70.0 4.6 %collective-permute-start.14 = (bf16[64,576]{1,0:T(8,128)(2,1)S(1)}, bf16[64,576]{1,0:T(8,128)(2,1)S(1)}, u32[]{:S(2)}, u32[]{:S(2)}) collective-permute-start(bf16[64,576]{1,0:T(8,128)(2,1)S(1)} %collective-permute-done.12), channel_id=1, source_target_pairs={{0,27},{1,0},{2,1},{3,2},{8,3},{9,8},{10,9},{11,10},{16,11},{17,16... | collective-permute-start | bytes 221192 | tf_op jit(solution)/shard_map/ppermute | solution.py:138
  74.7 1.4 collective-permute-done.14
  76.1 6.0 %collective-permute-done.15 = bf16[64,576]{1,0:T(8,128)(2,1)S(1)} collective-permute-done((bf16[64,576]{1,0:T(8,128)(2,1)S(1)}, bf16[64,576]{1,0:T(8,128)(2,1)S(1)}, u32[]{:S(2)}, u32[]{:S(2)}) %collective-permute-start.15) | collective-permute-done | bytes 73760 | tf_op jit(solution)/shard_map/ppermute | solution.py:133
  82.1 164.1 %conditional.1 = (bf16[1,1,64,64,512]{4,3,2,1,0:T(8,128)(2,1)S(1)}) conditional(s32[]{:T(128)} %convert_element_type.20, (s32[1,64]{1,0:T(1,128)}, s32[32]{0:T(128)}, bf16[4096,576]{0,1:T(8,128)(2,1)}, bf16[1,1,64,64,576]{4,3,2,1,0:T(8,128)(2,1)}, bf16[64,576]{1,0:T(8,128)(2,1)}, /*index=5*/s32[4,1]{0,1:T(1,128)S(1)}, s32[32]{0:T(128)}, ...), branch_computations={%region_1.5_spmd.clone, %region_5.10_spmd} | conditional | flops 3458017280 | bytes 202494112 | solution.py:157
  82.1 7.6 %copy.55 = bf16[4096,576]{1,0:T(8,128)(2,1)} copy(bf16[4096,576]{0,1:T(8,128)(2,1)} %get-tuple-element.740) | data formatting | bytes 9437184 | tf_op jit(solution)/shard_map
  89.7 5.4 %concatenate.14 = bf16[4352,576]{1,0:T(8,128)(2,1)} pad(bf16[4096,576]{1,0:T(8,128)(2,1)} %copy.55, bf16[]{:T(256)} %constant.137.clone.1), padding=0_256x0_0 | pad | bytes 9732098 | tf_op jit(solution)/shard_map/cond/branch_0_fun/concatenate | solution.py:58
  95.6 72.1 %gather_fusion = bf16[16384,576]{1,0:T(8,128)(2,1)} fusion(bf16[4352,576]{1,0:T(8,128)(2,1)} %concatenate.14, s32[16384]{0:T(1024)S(1)} %broadcast_clamp_fusion), kind=kCustom, calls=%fused_computation | custom fusion | bytes 37814272 | tf_op jit(solution)/shard_map/cond/branch_0_fun/jit(_take)/gather | solution.py:62
  167.8 18.1 %broadcast_select_fusion = bf16[64,256,576]{2,1,0:T(8,128)(2,1)} fusion(bf16[64,256,576]{2,1,0:T(8,128)(2,1)} %bitcast.97, pred[64,256]{1,0:T(8,128)(4,1)S(1)} %fusion.50), kind=kLoop, calls=%fused_computation.29 | loop fusion | flops 9437184 | bytes 37765120 | tf_op jit(solution)/shard_map/cond/branch_0_fun/jit(_take)/select_n | solution.py:62
  185.9 4.2 %fusion.30 = f32[64,1,64]{2,1,0:T(1,128)S(1)} fusion(bf16[1,1,64,64,576]{4,3,2,1,0:T(8,128)(2,1)} %get-tuple-element.277, bf16[64,576,1]{1,0,2:T(8,128)(2,1)S(1)} %bitcast.106), kind=kOutput, calls=%fused_computation.36 | convolution fusion | flops 4718592 | bytes 4808704 | tf_op jit(solution)/shard_map/cond/branch_0_fun/rhw,rw->rh/dot_general | solution.py:70
  190.1 2.0 copy.51
  192.3 0.7 dynamic_update_slice.99
  193.6 0.7 dynamic_update_slice.97
  194.3 0.7 dynamic_update_slice.96
  195.1 0.7 dynamic_update_slice.95
  195.8 0.7 dynamic_update_slice.94
  196.6 0.7 dynamic_update_slice.93
  197.4 0.7 dynamic_update_slice.92
  198.1 0.7 dynamic_update_slice.91
  198.9 0.7 dynamic_update_slice.90
  199.6 0.7 dynamic_update_slice.89
  200.4 0.7 dynamic_update_slice.88
  201.1 0.7 dynamic_update_slice.87
  201.9 0.7 dynamic_update_slice.86
  202.7 0.7 dynamic_update_slice.85
  203.4 0.7 dynamic_update_slice.84
  204.8 4.0 %multiply_bitcast_fusion.1 = f32[64,64,128]{2,1,0:T(8,128)S(1)} fusion(bf16[128,576,1]{1,0,2:T(8,128)(2,1)S(1)} %bitcast.102, bf16[1,1,64,64,576]{4,3,2,1,0:T(8,128)(2,1)} %get-tuple-element.277), kind=kOutput, calls=%fused_computation.49 | convolution fusion | flops 604504064 | bytes 6963200 | tf_op jit(solution)/shard_map/cond/branch_0_fun/rhw,kw->rhk/dot_general | solution.py:67
  208.8 13.1 %multiply_bitcast_fusion = f32[64,64,256]{2,1,0:T(8,128)} fusion(bf16[64,256,576]{2,1,0:T(8,128)(2,1)} %broadcast_select_fusion, bf16[1,1,64,64,576]{4,3,2,1,0:T(8,128)(2,1)} %get-tuple-element.277), kind=kOutput, calls=%fused_computation.45 | convolution fusion | flops 1209008128 | bytes 27787264 | tf_op jit(solution)/shard_map/cond/branch_0_fun/rhw,rtw->rht/dot_general | solution.py:64
  223.6 4.4 %fusion.58 = (f32[64,64]{1,0:T(8,128)S(1)}, f32[64,64,385]{2,1,0:T(8,128)S(1)}) fusion(f32[64,64,1]{2,1,0:T(8,128)} %copy.51, f32[64,64,128]{2,1,0:T(8,128)S(1)} %multiply_bitcast_fusion.1, f32[64,64,256]{2,1,0:T(8,128)} %multiply_bitcast_fusion, pred[64,385]{1,0:T(8,128)(4,1)S(1)} %add_add_fusion), kind=kOutput, calls=%fused_computation.74 | output fusion | flops 7885184 | bytes 12656704 | tf_op jit(solution)/shard_map/cond/branch_0_fun/sub | solution.py:23
  227.9 1.0 divide_convert_fusion.2
  229.0 12.1 %fusion.28 = f32[64,64,512]{2,1,0:T(8,128)} fusion(bf16[64,256,576]{2,1,0:T(8,128)(2,1)} %broadcast_select_fusion, bf16[64,64,385]{2,1,0:T(8,128)(2,1)S(1)} %divide_convert_fusion.2), kind=kOutput, calls=%fused_computation.30 | convolution fusion | flops 1073741824 | bytes 27262976 | tf_op jit(solution)/shard_map/cond/branch_0_fun/rht,rtl->rhl/dot_general | solution.py:82
  241.7 4.2 %fusion.37 = bf16[1,1,64,64,512]{4,3,2,1,0:T(8,128)(2,1)S(1)} fusion(f32[64,64,512]{2,1,0:T(8,128)} %fusion.28, f32[64,512]{1,0:T(8,128)S(1)} %slice_convert_fusion, f32[64,64]{1,0:T(8,128)S(1)} %convert_reduce_fusion, bf16[64,64,385]{2,1,0:T(8,128)(2,1)S(1)} %divide_convert_fusion.2, bf16[128,576]{1,0:T(8,128)(2,1)S(1)} %bitcast.103), kind=kOutput, calls=%fused_computation.43 | convolution fusion | flops 545259520 | bytes 13926400 | tf_op jit(solution)/shard_map/cond/branch_0_fun/rhk,kl->rhl/dot_general | solution.py:88
  246.2 2.0 copy-done.2
  (54 shorter events, 4.7 us)
Async XLA Ops:
  0.0 3.4 %collective-permute-start = (bf16[64,576]{1,0:T(8,128)(2,1)}, bf16[64,576]{1,0:T(8,128)(2,1)S(1)}, u32[]{:S(2)}, u32[]{:S(2)}) collective-permute-start(bf16[64,576]{1,0:T(8,128)(2,1)} %bitcast.104), channel_id=1, source_target_pairs={{0,4},{1,5},{2,6},{3,7},{8,12},{9,13},{10,14},{11,15},{16,20},{17,... | collective-permute-start | bytes 221192 | tf_op jit(solution)/shard_map/ppermute | solution.py:17
  3.4 8.7 %collective-permute-start.1 = (bf16[64,576]{1,0:T(8,128)(2,1)S(1)}, bf16[64,576]{1,0:T(8,128)(2,1)S(1)}, u32[]{:S(2)}, u32[]{:S(2)}) collective-permute-start(bf16[64,576]{1,0:T(8,128)(2,1)S(1)} %collective-permute-done), channel_id=1, source_target_pairs={{0,1},{1,2},{2,3},{3,8},{8,9},{9,10},{10,11},{11,16},{16,17},{17,1... | collective-permute-start | bytes 221192 | tf_op jit(solution)/shard_map/ppermute | solution.py:133
  5.5 6.6 %collective-permute-start.2 = (bf16[64,576]{1,0:T(8,128)(2,1)S(1)}, bf16[64,576]{1,0:T(8,128)(2,1)S(1)}, u32[]{:S(2)}, u32[]{:S(2)}) collective-permute-start(bf16[64,576]{1,0:T(8,128)(2,1)S(1)} %collective-permute-done), channel_id=1, source_target_pairs={{0,27},{1,0},{2,1},{3,2},{8,3},{9,8},{10,9},{11,10},{16,11},{17,16... | collective-permute-start | bytes 221192 | tf_op jit(solution)/shard_map/ppermute | solution.py:138
  12.1 7.0 %collective-permute-start.3 = (bf16[64,576]{1,0:T(8,128)(2,1)S(1)}, bf16[64,576]{1,0:T(8,128)(2,1)S(1)}, u32[]{:S(2)}, u32[]{:S(2)}) collective-permute-start(bf16[64,576]{1,0:T(8,128)(2,1)S(1)} %collective-permute-done.1), channel_id=1, source_target_pairs={{0,1},{1,2},{2,3},{3,8},{8,9},{9,10},{10,11},{11,16},{16,17},{17,1... | collective-permute-start | bytes 221192 | tf_op jit(solution)/shard_map/ppermute | solution.py:133
  12.1 7.0 %collective-permute-start.4 = (bf16[64,576]{1,0:T(8,128)(2,1)S(1)}, bf16[64,576]{1,0:T(8,128)(2,1)S(1)}, u32[]{:S(2)}, u32[]{:S(2)}) collective-permute-start(bf16[64,576]{1,0:T(8,128)(2,1)S(1)} %collective-permute-done.2), channel_id=1, source_target_pairs={{0,27},{1,0},{2,1},{3,2},{8,3},{9,8},{10,9},{11,10},{16,11},{17,16... | collective-permute-start | bytes 221192 | tf_op jit(solution)/shard_map/ppermute | solution.py:138
  19.0 7.0 %collective-permute-start.5 = (bf16[64,576]{1,0:T(8,128)(2,1)S(1)}, bf16[64,576]{1,0:T(8,128)(2,1)S(1)}, u32[]{:S(2)}, u32[]{:S(2)}) collective-permute-start(bf16[64,576]{1,0:T(8,128)(2,1)S(1)} %collective-permute-done.3), channel_id=1, source_target_pairs={{0,1},{1,2},{2,3},{3,8},{8,9},{9,10},{10,11},{11,16},{16,17},{17,1... | collective-permute-start | bytes 221192 | tf_op jit(solution)/shard_map/ppermute | solution.py:133
  19.1 9.3 %collective-permute-start.6 = (bf16[64,576]{1,0:T(8,128)(2,1)S(1)}, bf16[64,576]{1,0:T(8,128)(2,1)S(1)}, u32[]{:S(2)}, u32[]{:S(2)}) collective-permute-start(bf16[64,576]{1,0:T(8,128)(2,1)S(1)} %collective-permute-done.4), channel_id=1, source_target_pairs={{0,27},{1,0},{2,1},{3,2},{8,3},{9,8},{10,9},{11,10},{16,11},{17,16... | collective-permute-start | bytes 221192 | tf_op jit(solution)/shard_map/ppermute | solution.py:138
  26.0 7.3 %collective-permute-start.7 = (bf16[64,576]{1,0:T(8,128)(2,1)S(1)}, bf16[64,576]{1,0:T(8,128)(2,1)S(1)}, u32[]{:S(2)}, u32[]{:S(2)}) collective-permute-start(bf16[64,576]{1,0:T(8,128)(2,1)S(1)} %collective-permute-done.5), channel_id=1, source_target_pairs={{0,1},{1,2},{2,3},{3,8},{8,9},{9,10},{10,11},{11,16},{16,17},{17,1... | collective-permute-start | bytes 221192 | tf_op jit(solution)/shard_map/ppermute | solution.py:133
  28.3 6.5 %collective-permute-start.8 = (bf16[64,576]{1,0:T(8,128)(2,1)S(1)}, bf16[64,576]{1,0:T(8,128)(2,1)S(1)}, u32[]{:S(2)}, u32[]{:S(2)}) collective-permute-start(bf16[64,576]{1,0:T(8,128)(2,1)S(1)} %collective-permute-done.6), channel_id=1, source_target_pairs={{0,27},{1,0},{2,1},{3,2},{8,3},{9,8},{10,9},{11,10},{16,11},{17,16... | collective-permute-start | bytes 221192 | tf_op jit(solution)/shard_map/ppermute | solution.py:138
  33.4 7.0 %collective-permute-start.9 = (bf16[64,576]{1,0:T(8,128)(2,1)S(1)}, bf16[64,576]{1,0:T(8,128)(2,1)S(1)}, u32[]{:S(2)}, u32[]{:S(2)}) collective-permute-start(bf16[64,576]{1,0:T(8,128)(2,1)S(1)} %collective-permute-done.7), channel_id=1, source_target_pairs={{0,1},{1,2},{2,3},{3,8},{8,9},{9,10},{10,11},{11,16},{16,17},{17,1... | collective-permute-start | bytes 221192 | tf_op jit(solution)/shard_map/ppermute | solution.py:133
  34.9 18.2 %collective-permute-start.10 = (bf16[64,576]{1,0:T(8,128)(2,1)S(1)}, bf16[64,576]{1,0:T(8,128)(2,1)S(1)}, u32[]{:S(2)}, u32[]{:S(2)}) collective-permute-start(bf16[64,576]{1,0:T(8,128)(2,1)S(1)} %collective-permute-done.8), channel_id=1, source_target_pairs={{0,27},{1,0},{2,1},{3,2},{8,3},{9,8},{10,9},{11,10},{16,11},{17,16... | collective-permute-start | bytes 221192 | tf_op jit(solution)/shard_map/ppermute | solution.py:138
  40.4 17.5 %collective-permute-start.11 = (bf16[64,576]{1,0:T(8,128)(2,1)S(1)}, bf16[64,576]{1,0:T(8,128)(2,1)S(1)}, u32[]{:S(2)}, u32[]{:S(2)}) collective-permute-start(bf16[64,576]{1,0:T(8,128)(2,1)S(1)} %collective-permute-done.9), channel_id=1, source_target_pairs={{0,1},{1,2},{2,3},{3,8},{8,9},{9,10},{10,11},{11,16},{16,17},{17,1... | collective-permute-start | bytes 221192 | tf_op jit(solution)/shard_map/ppermute | solution.py:133
  53.1 16.9 %collective-permute-start.12 = (bf16[64,576]{1,0:T(8,128)(2,1)S(1)}, bf16[64,576]{1,0:T(8,128)(2,1)S(1)}, u32[]{:S(2)}, u32[]{:S(2)}) collective-permute-start(bf16[64,576]{1,0:T(8,128)(2,1)S(1)} %collective-permute-done.10), channel_id=1, source_target_pairs={{0,27},{1,0},{2,1},{3,2},{8,3},{9,8},{10,9},{11,10},{16,11},{17,16... | collective-permute-start | bytes 221192 | tf_op jit(solution)/shard_map/ppermute | solution.py:138
  57.9 16.7 %collective-permute-start.13 = (bf16[64,576]{1,0:T(8,128)(2,1)S(1)}, bf16[64,576]{1,0:T(8,128)(2,1)S(1)}, u32[]{:S(2)}, u32[]{:S(2)}) collective-permute-start(bf16[64,576]{1,0:T(8,128)(2,1)S(1)} %collective-permute-done.11), channel_id=1, source_target_pairs={{0,1},{1,2},{2,3},{3,8},{8,9},{9,10},{10,11},{11,16},{16,17},{17,1... | collective-permute-start | bytes 221192 | tf_op jit(solution)/shard_map/ppermute | solution.py:133
  70.0 6.1 %collective-permute-start.14 = (bf16[64,576]{1,0:T(8,128)(2,1)S(1)}, bf16[64,576]{1,0:T(8,128)(2,1)S(1)}, u32[]{:S(2)}, u32[]{:S(2)}) collective-permute-start(bf16[64,576]{1,0:T(8,128)(2,1)S(1)} %collective-permute-done.12), channel_id=1, source_target_pairs={{0,27},{1,0},{2,1},{3,2},{8,3},{9,8},{10,9},{11,10},{16,11},{17,16... | collective-permute-start | bytes 221192 | tf_op jit(solution)/shard_map/ppermute | solution.py:138
  74.6 7.5 %collective-permute-start.15 = (bf16[64,576]{1,0:T(8,128)(2,1)S(1)}, bf16[64,576]{1,0:T(8,128)(2,1)S(1)}, u32[]{:S(2)}, u32[]{:S(2)}) collective-permute-start(bf16[64,576]{1,0:T(8,128)(2,1)S(1)} %collective-permute-done.13), channel_id=1, source_target_pairs={{0,1},{1,2},{2,3},{3,8},{8,9},{9,10},{10,11},{11,16},{16,17},{17,1... | collective-permute-start | bytes 221192 | tf_op jit(solution)/shard_map/ppermute | solution.py:133
  89.7 5.4 %copy-start.4 = (s32[1,64]{1,0:T(1,128)S(1)}, s32[1,64]{1,0:T(1,128)}, u32[]{:S(2)}) copy-start(s32[1,64]{1,0:T(1,128)} %get-tuple-element.278) | copy-start | bytes 772 | tf_op jit(solution)/shard_map/cond
  167.8 18.2 %copy-start.3 = (bf16[64,576]{1,0:T(8,128)(2,1)S(1)}, bf16[64,576]{1,0:T(8,128)(2,1)}, u32[]{:S(2)}) copy-start(bf16[64,576]{1,0:T(8,128)(2,1)} %get-tuple-element.276) | copy-start | bytes 221188 | tf_op jit(solution)/shard_map/cond
  208.8 13.1 %copy-start.1 = (s32[32]{0:T(128)S(1)}, s32[32]{0:T(128)}, u32[]{:S(2)}) copy-start(s32[32]{0:T(128)} %get-tuple-element.305) | copy-start | bytes 388 | tf_op jit(solution)/shard_map/cond
  208.8 13.8 %copy-start = (s32[32]{0:T(128)S(1)}, s32[32]{0:T(128)}, u32[]{:S(2)}) copy-start(s32[32]{0:T(128)} %get-tuple-element.287) | copy-start | bytes 388 | tf_op jit(solution)/shard_map/cond
  246.2 2.0 copy-start.2
